TPU v7x, 256 devices: a whole 4x4x8 slice. The times are simulated.
256 devices in a mesh: exp: 32 (over y, z_hi, core), hid: 8 (over z_lo, x).
Axes of the slice: x: 4, y: 4, z: 8 (z_hi: 4, z_lo: 2; z = z_hi * 2 + z_lo), core: 2. Of those that a mesh axis runs over, the one named last changes fastest.
Arguments:
- tokens: bfloat16 [1024, 2048], P(('exp', 'hid')), may hold values from -6 to 6
- grad_out: bfloat16 [1024, 2048], P(('exp', 'hid')), may hold values from -3 to 3
- router_logits: float32 [1024, 128], P(('exp', 'hid')), may hold values from -12 to 330
- selected: int32 [1024, 8], P(('exp', 'hid')), may hold values from 0 to 127, as said below
- router_w: bfloat16 [2048, 128], replicated, may hold values from -0.59765625 to 0.59765625
- w_gate: bfloat16 [256, 2048, 384], P(('exp', 'hid')), may hold values from -0.125 to 0.125
- w_up: bfloat16 [256, 2048, 384], P(('exp', 'hid')), may hold values from -0.125 to 0.125
- w_down: bfloat16 [256, 384, 2048], P(('exp', 'hid')), may hold values from -0.21875 to 0.21875
Outputs:
- x_grad: bfloat16 [1024, 2048], P(('exp', 'hid'))
- router_grad: float32 [2048, 128], P(('exp', 'hid'))
Inputs may be any that keep to these rules, and one draw needn't show every extreme that they name: `selected`: each row names 8 different experts; within each aligned block of 32 rows (the tokens of one index of exp) no expert is named by more than 4 rows, and in every block some expert is named by exactly 4 rows.
All inputs are finite; a program needn't handle non-finite values.
Results may differ from a plain program's by a relative error of at most 0.0075.
Values may be sent and summed in bfloat16 or wider, within the bound.
A program may use at most 64 MiB of HBM per device.

v0:
```python
import jax
import jax.numpy as jnp
from jax import lax
from jax.sharding import PartitionSpec as P


def softmax_rows(values):
    top_val = jnp.max(values, axis=-1, keepdims=True)
    raised = jnp.exp(values - top_val)
    return raised / jnp.sum(raised, axis=-1, keepdims=True)


def combine_table(logits, chosen, expert_count):
    picked = jnp.take_along_axis(logits, chosen, axis=1)
    weights = softmax_rows(picked)
    expert_ids = jnp.arange(expert_count, dtype=jnp.int32)
    matched = (chosen[:, :, None] == expert_ids[None, None, :]).astype(jnp.float32)
    return jnp.sum(weights[:, :, None] * matched, axis=1).astype(jnp.bfloat16)


def unit_terms(x_rows, g_rows, c_rows, w_gate, w_up, w_down, unit_pick):
    gate_pre = jnp.einsum("td,udf->utf", x_rows, w_gate, preferred_element_type=jnp.float32)
    up_pre = jnp.einsum("td,udf->utf", x_rows, w_up, preferred_element_type=jnp.float32)
    back_grad = jnp.einsum("td,ufd->utf", g_rows, w_down, preferred_element_type=jnp.float32)
    sig_gate = jax.nn.sigmoid(gate_pre)
    act_gate = gate_pre * sig_gate
    score_part = jnp.sum(act_gate * up_pre * back_grad, axis=2).T
    column_rows = jnp.dot(c_rows, unit_pick, preferred_element_type=jnp.float32)
    weighted = column_rows.T[:, :, None] * back_grad
    grad_gate = (weighted * up_pre * sig_gate * (1.0 + gate_pre * (1.0 - sig_gate))).astype(
        jnp.bfloat16
    )
    grad_up = (weighted * act_gate).astype(jnp.bfloat16)
    input_part = jnp.einsum("utf,udf->td", grad_gate, w_gate, preferred_element_type=jnp.float32)
    input_part = input_part + jnp.einsum(
        "utf,udf->td", grad_up, w_up, preferred_element_type=jnp.float32
    )
    return (score_part, input_part, column_rows)


def on_device(tokens, grad_out, router_logits, selected, router_w, w_gate, w_up, w_down):
    tok_local, model_width = tokens.shape
    unit_count = w_gate.shape[0]
    expert_count = router_logits.shape[1]
    spread_exp = lax.axis_size("exp")
    spread_hid = lax.axis_size("hid")
    own_block = lax.axis_index(("exp", "hid"))
    unit_expert = (own_block * unit_count + jnp.arange(unit_count, dtype=jnp.int32)) // 2
    expert_ids = jnp.arange(expert_count, dtype=jnp.int32)
    unit_pick = (expert_ids[:, None] == unit_expert[None, :]).astype(jnp.bfloat16)
    combine = combine_table(router_logits, selected, expert_count)
    score_part, input_part, column_rows = unit_terms(
        lax.all_gather(tokens, ("exp", "hid"), axis=0, tiled=True),
        lax.all_gather(grad_out, ("exp", "hid"), axis=0, tiled=True),
        lax.all_gather(combine, ("exp", "hid"), axis=0, tiled=True),
        w_gate,
        w_up,
        w_down,
        unit_pick,
    )
    input_all = input_part
    used_all = column_rows
    scores, input_all, used_all = (score_part, input_all, used_all)
    input_sum = lax.psum_scatter(input_all, ("exp", "hid"), scatter_dimension=0, tiled=True)
    shaped = scores.reshape(spread_exp, spread_hid, tok_local, 1, unit_count)
    arrived = lax.all_to_all(
        lax.all_to_all(shaped, "exp", split_axis=0, concat_axis=3, tiled=True),
        "hid",
        split_axis=1,
        concat_axis=4,
        tiled=True,
    )
    expert_scores = jnp.sum(arrived.reshape(tok_local, expert_count, 2), axis=2)
    probs_all = softmax_rows(router_logits)
    mean_score = jnp.sum(probs_all * expert_scores, axis=1, keepdims=True)
    logit_grad = (probs_all * (expert_scores - mean_score)).astype(jnp.bfloat16)
    router_grad = lax.psum_scatter(
        jnp.einsum("tc,te->ce", tokens, logit_grad, preferred_element_type=jnp.float32),
        ("exp", "hid"),
        scatter_dimension=0,
        tiled=True,
    )
    router_part = jnp.einsum("te,de->td", logit_grad, router_w, preferred_element_type=jnp.float32)
    x_grad = (input_sum + router_part).astype(jnp.bfloat16)
    return (x_grad, router_grad)


def solution(mesh):
    placed = (
        P(("exp", "hid"), None),
        P(("exp", "hid"), None),
        P(("exp", "hid"), None),
        P(("exp", "hid"), None),
        P(),
        P(("exp", "hid"), None, None),
        P(("exp", "hid"), None, None),
        P(("exp", "hid"), None, None),
    )
    return jax.shard_map(
        on_device,
        mesh=mesh,
        in_specs=placed,
        out_specs=(P(("exp", "hid"), None), P(("exp", "hid"), None)),
        check_vma=False,
    )
```

profile of v0, /device:TPU:97, one launch (start us, length us, event | category | flops | bytes accessed | tf_op | source)
XLA Modules:
  0.0 1772.1 jit_solution(1746545466882803414)
XLA Ops:
  7.2 0.0 copy-start
  7.2 0.0 copy-start.6
  7.2 0.0 copy-start.1
  7.2 0.0 all-gather.8.cloned.1.call-start
  7.2 0.7 all-gather.8.cloned.1.call-update
  7.9 0.0 all-gather.6.cloned.1.call-start
  8.0 0.7 all-gather.6.cloned.1.call-update
  8.7 0.7 bitcast_or_fusion
  9.4 0.1 reshape.86
  9.5 1.4 gather_fusion
  10.9 0.1 reshape.89
  11.0 0.0 copy-done.1
  11.0 0.1 reduce_max.19
  11.1 0.2 fusion.30
  11.3 0.0 copy-done.6
  11.3 0.1 fusion.35
  11.4 0.2 fusion.28
  11.6 0.1 fusion.27
  11.7 0.1 select_reduce_fusion
  11.8 561.5 %all-gather = bf16[256,4,128]{2,1,0:T(4,128)(2,1)S(1)} all-gather(bf16[1,4,128]{2,1,0:T(4,128)(2,1)S(1)} %bitcast.132), channel_id=1, replica_groups=mesh['exp'=32,'hid'=8] {'exp','hid'}, dimensions={0}, use_global_device_ids=true | all-gather | bytes 263168 | tf_op jit(solution)/shard_map/all_gather | solution.py:55
  573.3 0.2 fusion.24
  573.5 150.6 %all-gather.8.cloned.1.call-done = bf16[256,4,2048]{2,1,0:T(4,128)(2,1)} async-done(((bf16[1,4,2048]{2,1,0:T(4,128)(2,1)}), bf16[256,4,2048]{2,1,0:T(4,128)(2,1)}) %all-gather.8.cloned.1.call-update) | async-done | bytes 4194320 | tf_op jit(solution)/shard_map/all_gather | solution.py:53
  724.0 6.9 reshape.102
  730.9 0.0 copy-done
  730.9 0.0 copy-start.2
  730.9 0.0 copy-start.3
  731.0 4.2 fusion.11
  735.1 0.0 copy-done.2
  735.1 0.0 copy-done.3
  735.1 3.0 fusion.14
  738.1 693.5 %all-gather.6.cloned.1.call-done = bf16[256,4,2048]{2,1,0:T(4,128)(2,1)} async-done(((bf16[1,4,2048]{2,1,0:T(4,128)(2,1)}), bf16[256,4,2048]{2,1,0:T(4,128)(2,1)}) %all-gather.6.cloned.1.call-update) | async-done | bytes 4194320 | tf_op jit(solution)/shard_map/all_gather | solution.py:54
  1431.6 6.9 reshape.100
  1438.5 6.2 fusion.1
  1444.8 0.1 reshape_transpose.3
  1444.9 0.9 copy.38
  1445.8 7.2 all-to-all-start
  1453.0 7.9 fusion.9
  1460.8 0.2 all-to-all-done
  1461.0 0.1 copy.39
  1461.1 0.5 broadcast.72
  1461.6 0.7 reduce.1
  1462.3 0.7 reshape.107
  1463.0 4.0 all-to-all-start.1
  1467.0 0.0 copy-start.5
  1467.0 0.0 all-reduce.5.cloned.1.call-start
  1467.0 10.0 convolution_add_fusion
  1477.0 0.0 all-to-all-done.1
  1477.0 0.7 reduce.2
  1477.7 0.1 reshape.108
  1477.8 0.1 copy.41
  1477.9 0.2 reduce_sum.58
  1478.1 0.1 copy.43
  1478.2 0.2 multiply_reduce_fusion
  1478.4 0.1 multiply_convert_fusion.1
  1478.5 0.0 copy-done.5
  1478.5 1.4 convolution_bitcast_fusion
  1479.9 0.0 copy-start.4
  1479.9 0.0 all-reduce.5.cloned.1.call-update
  1479.9 282.4 %all-reduce.5.cloned.1.call-done = (f32[1024,2048]{1,0:T(8,128)}, f32[2048,128]{0,1:T(8,128)}) async-done(((f32[1024,2048]{1,0:T(8,128)}, f32[2048,128]{0,1:T(8,128)}), (f32[1024,2048]{1,0:T(8,128)}, f32[2048,128]{0,1:T(8,128)})) %all-reduce.5.cloned.1.call-update) | async-done | bytes 9437200
  1762.3 0.9 constant_dynamic-slice_fusion
  1763.2 0.7 copy.44
  1763.9 0.0 copy-done.4
  1763.9 1.7 fusion
  (1 shorter events, 0.0 us)
Async XLA Ops:
  7.2 723.8 %copy-start = (bf16[1,2048,384]{2,1,0:T(8,128)(2,1)S(1)}, bf16[1,2048,384]{2,1,0:T(8,128)(2,1)}, u32[]{:S(2)}) copy-start(bf16[1,2048,384]{2,1,0:T(8,128)(2,1)} %param.13) | copy-start | bytes 4718596
  7.2 4.1 copy-start.6
  7.2 3.8 copy-start.1
  7.2 716.8 %all-gather.8.cloned.1.call-start = ((), (), s32[]{:S(2)}) async-start(), calls=%async_computation.3 | async-start | bytes 4210688 | tf_op jit(solution)/shard_map/all_gather | solution.py:53
  7.9 1423.7 %all-gather.6.cloned.1.call-start = ((), (), s32[]{:S(2)}) async-start(), calls=%async_computation.2 | async-start | bytes 4210688 | tf_op jit(solution)/shard_map/all_gather | solution.py:54
  730.9 4.2 copy-start.2
  730.9 4.2 copy-start.3
  1445.8 15.2 all-to-all-start
  1463.0 14.0 all-to-all-start.1
  1467.0 11.5 copy-start.5
  1467.0 295.3 %all-reduce.5.cloned.1.call-start = ((), (), s32[]{:S(2)}) async-start(), calls=%async_computation.4 | async-start | bytes 18874368
  1479.9 284.1 %copy-start.4 = (bf16[2048,128]{1,0:T(8,128)(2,1)S(1)}, bf16[2048,128]{1,0:T(8,128)(2,1)}, u32[]{:S(2)}) copy-start(bf16[2048,128]{1,0:T(8,128)(2,1)} %param.12) | copy-start | bytes 1572868
Sparse Core Ops, SparseCore 0:
  9.9 714.0 all-gather.7
  725.9 705.6 all-gather.5
  1480.0 282.2 all-reduce.4
where the time goes:
time: 1770 us
  waiting for transfers between devices  1130 us (64%)
  blocking collectives  562 us (32%)
  matrix products  34.6 us (2%)
  local copies, waits for them, and re-layouts  19.6 us (1%)
    all_gather x1, waiting for transfers between devices, on_device(): lax.all_gather(grad_out, ('exp', 'hid'), axis=0, tiled=True)  693 us
    all_gather x1, blocking collectives, on_device(): lax.all_gather(combine, ('exp', 'hid'), axis=0, tiled=True)  562 us
    unnamed x4, waiting for transfers between devices  284 us
    all_gather x1, waiting for transfers between devices, on_device(): lax.all_gather(tokens, ('exp', 'hid'), axis=0, tiled=True)  151 us
  transfers between devices with their start and end apart: 5, of which 4 were waited for; matrix products, arithmetic and copies ran while one was open for 2% of the time, Pallas kernels for 0%

commit v1 on v0

--- a/solution.py
+++ b/solution.py
@@ -2,6 +2,11 @@
 import jax.numpy as jnp
 from jax import lax
 from jax.sharding import PartitionSpec as P
+
+
+def swapped_in(block, mesh_axis, along):
+    sent = jnp.stack([block] * lax.axis_size(mesh_axis))
+    return jnp.concatenate(lax.all_to_all(sent, mesh_axis, 0, 0), axis=along)
 
 
 def softmax_rows(values):
@@ -50,7 +55,7 @@
     unit_pick = (expert_ids[:, None] == unit_expert[None, :]).astype(jnp.bfloat16)
     combine = combine_table(router_logits, selected, expert_count)
     score_part, input_part, column_rows = unit_terms(
-        lax.all_gather(tokens, ("exp", "hid"), axis=0, tiled=True),
+        swapped_in(tokens, ("exp", "hid"), 0),
         lax.all_gather(grad_out, ("exp", "hid"), axis=0, tiled=True),
         lax.all_gather(combine, ("exp", "hid"), axis=0, tiled=True),
         w_gate,

time: 1770 us -> 1100 us (0.62)
  waiting for transfers between devices: 1130 us -> 365 us
  blocking collectives: 562 us -> 633 us
    all_gather x1, waiting for transfers between devices: 693 us -> 82.3 us  [on_device(): lax.all_gather(grad_out, ('exp', 'hid'), axis=0, tiled=True)]
    all_gather x1 -> x0, waiting for transfers between devices: 151 us -> none  [on_device(): lax.all_gather(tokens, ('exp', 'hid'), axis=0, tiled=True)]
    all_gather x1, blocking collectives: 562 us -> 633 us  [on_device(): lax.all_gather(combine, ('exp', 'hid'), axis=0, tiled=True)]
    unnamed x4 -> x3, waiting for transfers between devices: 284 us -> 283 us
  transfers between devices with their start and end apart: 5 -> 5, of which waited for: 4 -> 2; matrix products, arithmetic and copies ran while one was open for 2% -> 3% of each run, Pallas kernels for 0% -> 0%
where the time goes in v1:
time: 1100 us
  blocking collectives  633 us (58%)
  waiting for transfers between devices  365 us (33%)
  matrix products  34.6 us (3%)
  starting transfers between devices  26.7 us (2%)
  local copies, waits for them, and re-layouts  23.9 us (2%)
  between operations  14.2 us (1%)
    all_gather x1, blocking collectives, on_device(): lax.all_gather(combine, ('exp', 'hid'), axis=0, tiled=True)  633 us
    unnamed x3, waiting for transfers between devices  283 us
    all_gather x1, waiting for transfers between devices, on_device(): lax.all_gather(grad_out, ('exp', 'hid'), axis=0, tiled=True)  82.3 us
  transfers between devices with their start and end apart: 5, of which 2 were waited for; matrix products, arithmetic and copies ran while one was open for 3% of the time, Pallas kernels for 0%

profile of v1, /device:TPU:97, one launch (start us, length us, event | category | flops | bytes accessed | tf_op | source)
XLA Modules:
  0.0 1100.2 jit_solution(15828011046348913139)
XLA Ops:
  7.2 0.0 copy-start
  7.2 4.9 stack.2
  12.1 0.0 copy-start.6
  12.1 0.0 copy-start.1
  12.1 15.3 %all-to-all-start = ((bf16[256,4,2048]{2,1,0:T(4,128)(2,1)}), bf16[256,4,2048]{2,1,0:T(4,128)(2,1)}, u32[]{:S(2)}, u32[]{:S(2)}) async-start(bf16[256,4,2048]{2,1,0:T(4,128)(2,1)} %stack.2), calls=%async_computation | async-start | bytes 8388608 | tf_op jit(solution)/shard_map/all_to_all | solution.py:9
  27.5 0.0 all-gather.4.cloned.1.call-start
  27.5 0.7 all-gather.4.cloned.1.call-update
  28.2 0.0 copy-done.6
  28.2 0.1 reshape.92
  28.3 0.0 copy-done.1
  28.3 0.8 gather_fusion
  29.1 0.1 reshape.95
  29.2 0.1 reduce_max.19
  29.3 0.2 fusion.30
  29.5 0.1 fusion.35
  29.6 0.2 fusion.28
  29.8 0.1 fusion.27
  29.8 0.1 select_reduce_fusion
  29.9 632.8 %all-gather = bf16[256,4,128]{2,1,0:T(4,128)(2,1)S(1)} all-gather(bf16[1,4,128]{2,1,0:T(4,128)(2,1)S(1)} %bitcast.130), channel_id=1, replica_groups=mesh['exp'=32,'hid'=8] {'exp','hid'}, dimensions={0}, use_global_device_ids=true | all-gather | bytes 263168 | tf_op jit(solution)/shard_map/all_gather | solution.py:60
  662.8 0.2 fusion.24
  662.9 0.0 all-to-all-done
  662.9 7.0 reshape.87
  669.9 0.0 copy-done
  669.9 0.0 copy-start.2
  669.9 0.0 copy-start.3
  669.9 4.2 fusion.11
  674.1 0.0 copy-done.2
  674.1 0.0 copy-done.3
  674.1 3.0 fusion.14
  677.1 82.3 %all-gather.4.cloned.1.call-done = bf16[256,4,2048]{2,1,0:T(4,128)(2,1)} async-done(((bf16[1,4,2048]{2,1,0:T(4,128)(2,1)}), bf16[256,4,2048]{2,1,0:T(4,128)(2,1)}) %all-gather.4.cloned.1.call-update) | async-done | bytes 4194320 | tf_op jit(solution)/shard_map/all_gather | solution.py:59
  759.4 6.9 reshape.106
  766.3 6.2 fusion.1
  772.6 0.1 reshape_transpose.3
  772.7 0.9 copy.38
  773.6 5.2 all-to-all-start.1
  778.8 7.9 fusion.9
  786.6 0.0 all-to-all-done.1
  786.7 0.1 copy.39
  786.8 0.5 broadcast.74
  787.3 0.7 reduce.1
  788.0 0.7 reshape.111
  788.7 6.1 all-to-all-start.2
  794.8 0.0 copy-start.5
  794.8 0.0 all-reduce.5.cloned.1.call-start
  794.8 10.0 convolution_add_fusion
  804.9 0.0 all-to-all-done.2
  804.9 0.7 reduce.2
  805.5 0.1 reshape.112
  805.6 0.1 copy.41
  805.8 0.2 reduce_sum.58
  805.9 0.1 copy.43
  806.0 0.2 multiply_reduce_fusion
  806.2 0.1 multiply_convert_fusion.1
  806.3 0.0 copy-done.5
  806.3 1.4 convolution_bitcast_fusion
  807.7 0.0 copy-start.4
  807.7 0.0 all-reduce.5.cloned.1.call-update
  807.7 282.3 %all-reduce.5.cloned.1.call-done = (f32[1024,2048]{1,0:T(8,128)}, f32[2048,128]{0,1:T(8,128)}) async-done(((f32[1024,2048]{1,0:T(8,128)}, f32[2048,128]{0,1:T(8,128)}), (f32[1024,2048]{1,0:T(8,128)}, f32[2048,128]{0,1:T(8,128)})) %all-reduce.5.cloned.1.call-update) | async-done | bytes 9437200
  1090.0 0.9 constant_dynamic-slice_fusion
  1091.0 0.7 copy.44
  1091.6 0.0 copy-done.4
  1091.6 1.7 fusion
  (2 shorter events, 0.0 us)
Async XLA Ops:
  7.2 662.7 %copy-start = (bf16[1,2048,384]{2,1,0:T(8,128)(2,1)S(1)}, bf16[1,2048,384]{2,1,0:T(8,128)(2,1)}, u32[]{:S(2)}) copy-start(bf16[1,2048,384]{2,1,0:T(8,128)(2,1)} %param.13) | copy-start | bytes 4718596
  12.1 16.1 %copy-start.6 = (s32[4,8]{1,0:T(4,128)S(1)}, s32[4,8]{1,0:T(4,128)}, u32[]{:S(2)}) copy-start(s32[4,8]{1,0:T(4,128)} %param.11) | copy-start | bytes 388
  12.1 16.2 %copy-start.1 = (f32[4,128]{1,0:T(4,128)S(1)}, f32[4,128]{1,0:T(4,128)}, u32[]{:S(2)}) copy-start(f32[4,128]{1,0:T(4,128)} %param.10) | copy-start | bytes 6148
  12.1 650.8 %all-to-all-start = ((bf16[256,4,2048]{2,1,0:T(4,128)(2,1)}), bf16[256,4,2048]{2,1,0:T(4,128)(2,1)}, u32[]{:S(2)}, u32[]{:S(2)}) async-start(bf16[256,4,2048]{2,1,0:T(4,128)(2,1)} %stack.2), calls=%async_computation | async-start | bytes 8388608 | tf_op jit(solution)/shard_map/all_to_all | solution.py:9
  27.5 732.0 %all-gather.4.cloned.1.call-start = ((), (), s32[]{:S(2)}) async-start(), calls=%async_computation.3 | async-start | bytes 4210688 | tf_op jit(solution)/shard_map/all_gather | solution.py:59
  669.9 4.2 copy-start.2
  669.9 4.2 copy-start.3
  773.6 13.1 %all-to-all-start.1 = ((f32[32,8,4,1,1]{1,2,4,3,0:T(4,128)}), f32[32,8,4,1,1]{1,2,4,3,0:T(4,128)S(1)}, u32[]{:S(2)}, u32[]{:S(2)}) async-start(f32[32,8,4,1,1]{1,2,4,3,0:T(4,128)} %copy.38), calls=%async_computation.1 | async-start | bytes 131072 | tf_op jit(solution)/shard_map/all_to_all | solution.py:72
  788.7 16.2 %all-to-all-start.2 = ((f32[8,1,128]{2,1,0:T(1,128)}), f32[8,1,128]{2,1,0:T(1,128)S(1)}, u32[]{:S(2)}, u32[]{:S(2)}) async-start(f32[8,1,128]{2,1,0:T(1,128)} %reshape.111), calls=%async_computation.2 | async-start | bytes 8192 | tf_op jit(solution)/shard_map/all_to_all | solution.py:71
  794.8 11.5 %copy-start.5 = (bf16[4,2048]{1,0:T(4,128)(2,1)S(1)}, bf16[4,2048]{1,0:T(4,128)(2,1)}, u32[]{:S(2)}) copy-start(bf16[4,2048]{1,0:T(4,128)(2,1)} %param.8) | copy-start | bytes 49156
  794.8 295.2 %all-reduce.5.cloned.1.call-start = ((), (), s32[]{:S(2)}) async-start(), calls=%async_computation.4 | async-start | bytes 18874368
  807.7 284.0 %copy-start.4 = (bf16[2048,128]{1,0:T(8,128)(2,1)S(1)}, bf16[2048,128]{1,0:T(8,128)(2,1)}, u32[]{:S(2)}) copy-start(bf16[2048,128]{1,0:T(8,128)(2,1)} %param.12) | copy-start | bytes 1572868
Sparse Core Ops, SparseCore 0:
  30.2 729.2 all-gather.3
  807.8 282.1 all-reduce.4
